TPU v7x, 32 devices: a whole 2x2x4 slice. The times are simulated.
32 devices in a mesh: clip: 4 (over x, core), tm: 8 (over z, y).
Axes of the slice: x: 2, y: 2, z: 4, core: 2. Of those that a mesh axis runs over, the one named last changes fastest.
Arguments:
- inputs: bfloat16 [4, 2560, 768], P('clip', 'tm'), may hold values from -6 to 6
- query_states: bfloat16 [4, 2560, 768], P('clip', 'tm'), may hold values from -9 to 9
- key_states: bfloat16 [4, 2560, 768], P('clip', 'tm'), may hold values from -9 to 9
- value_states: bfloat16 [4, 2560, 768], P('clip', 'tm'), may hold values from -6 to 6
- out_grad: bfloat16 [4, 2560, 768], P('clip', 'tm'), may hold values from -1.1953125 to 1.1953125
- first_flags: int32 [4, 8], P('clip'), may hold values from 0 to 1, as said below
- weight: float32 [768, 768], P('tm'), may hold values from -1.2 to 1.2
- moment_one: float32 [768, 768], P('tm'), may hold values from -6 to 6
- moment_two: float32 [768, 768], P('tm'), may hold values from 0.25 to 4
Outputs:
- new_weight: float32 [768, 768], P('tm')
- new_moment_one: float32 [768, 768], P('tm')
- new_moment_two: float32 [768, 768], P('tm')
Inputs may be any that keep to these rules, and one draw needn't show every extreme that they name: `first_flags`: the first frame of every sequence has flag 1.
All inputs are finite; a program needn't handle non-finite values.
Results may differ from a plain program's by a relative error of at most 0.0044.
Values may be sent and summed in bfloat16 or wider, within the bound.
No kernel may reach another device: no remote copies, remote signals or barrier semaphores. Data moves between devices by JAX's collectives and lax.ppermute only.
A program may use at most 64 MiB of HBM per device.

v0:
```python
import math
import jax
import jax.numpy as jnp
from jax import lax
from jax.sharding import PartitionSpec as P

HEAD_DIM = 128
beta_one = 0.9
beta_two = 0.95
learn_rate = 0.001
adam_eps = 1e-08
decay_rate = 0.1
step_count = 10.0


def from_behind(value, axis, steps):
    count = lax.axis_size(axis)
    leading, last = (max(0, -steps), min(count, count - steps))
    return lax.ppermute(value, axis, [(source, source + steps) for source in range(leading, last)])


def adamw(weight, moment_one, moment_two, gradient):
    new_one = beta_one * moment_one + (1.0 - beta_one) * gradient
    new_two = beta_two * moment_two + (1.0 - beta_two) * gradient * gradient
    corr_one = new_one / (1.0 - beta_one**step_count)
    corr_two = new_two / (1.0 - beta_two**step_count)
    new_weight = weight - learn_rate * (
        corr_one / (jnp.sqrt(corr_two) + adam_eps) + decay_rate * weight
    )
    return (new_weight, new_one, new_two)


def window_grad(query_rows, key_window, value_window, grad_rows, allowed):
    tok_rows = query_rows.shape[0]
    head_size = HEAD_DIM
    head_count = query_rows.shape[1] // head_size
    scaling = 1.0 / math.sqrt(head_size)
    query_heads = query_rows.reshape(tok_rows, head_count, head_size)
    key_heads = key_window.reshape(3 * tok_rows, head_count, head_size)
    value_heads = value_window.reshape(3 * tok_rows, head_count, head_size)
    grad_heads = grad_rows.reshape(tok_rows, head_count, head_size)
    scores = (
        jnp.einsum("qhd,khd->hqk", query_heads, key_heads, preferred_element_type=jnp.float32)
        * scaling
    )
    scores = jnp.where(allowed[None, None, :], scores, -jnp.inf)
    row_max = jnp.max(scores, axis=-1, keepdims=True)
    raised = jnp.exp(scores - row_max)
    softmax = raised / jnp.sum(raised, axis=-1, keepdims=True)
    dprobs = jnp.einsum("qhd,khd->hqk", grad_heads, value_heads, preferred_element_type=jnp.float32)
    row_dot = jnp.sum(softmax * dprobs, axis=-1, keepdims=True)
    dscores = (softmax * (dprobs - row_dot) * scaling).astype(jnp.bfloat16)
    window_part = jnp.einsum(
        "hqk,qhd->khd", dscores, query_heads, preferred_element_type=jnp.float32
    )
    return window_part.reshape(3 * tok_rows, head_count * head_size)


def contract_rows(features, key_grad):
    return lax.dot_general(
        features, key_grad, (((0,), (0,)), ((), ())), preferred_element_type=jnp.float32
    )


def body(
    inputs,
    query_states,
    key_states,
    value_states,
    out_grad,
    first_flags,
    weight,
    moment_one,
    moment_two,
):
    tok_rows = inputs.shape[1]
    position = lax.axis_index("tm")
    flag_row = first_flags[0]
    own_flag = flag_row[position]
    prev_flag = jnp.where(position >= 1, flag_row[jnp.maximum(position - 1, 0)], 1)
    near_ok = own_flag == 0
    far_ok = jnp.logical_and(near_ok, prev_flag == 0)
    allowed = jnp.concatenate(
        [
            jnp.broadcast_to(far_ok, (tok_rows,)),
            jnp.broadcast_to(near_ok, (tok_rows,)),
            jnp.ones((tok_rows,), bool),
        ]
    )
    queries = query_states[0]
    keys_own = key_states[0]
    values_own = value_states[0]
    near_keys, near_values = from_behind((keys_own, values_own), "tm", 1)
    far_keys, far_values = from_behind((keys_own, values_own), "tm", 2)
    key_window = jnp.concatenate([far_keys, near_keys, keys_own], axis=0)
    value_window = jnp.concatenate([far_values, near_values, values_own], axis=0)
    window_part = window_grad(queries, key_window, value_window, out_grad[0], allowed)
    far_part = window_part[:tok_rows]
    near_part = window_part[tok_rows : 2 * tok_rows]
    own_part = window_part[2 * tok_rows :]
    from_next = from_behind(near_part, "tm", -1)
    from_after = from_behind(far_part, "tm", -2)
    summed = own_part + from_next + from_after
    key_grad = summed.astype(jnp.bfloat16)
    features = inputs[0]
    local_rows = lax.psum_scatter(
        contract_rows(features, key_grad), "tm", scatter_dimension=0, tiled=True
    )
    gradient = lax.psum(local_rows, "clip")
    return adamw(weight, moment_one, moment_two, gradient)


def solution(mesh):
    in_specs = (
        P("clip", "tm", None),
        P("clip", "tm", None),
        P("clip", "tm", None),
        P("clip", "tm", None),
        P("clip", "tm", None),
        P("clip", None),
        P("tm", None),
        P("tm", None),
        P("tm", None),
    )
    out_specs = (P("tm", None), P("tm", None), P("tm", None))
    return jax.shard_map(body, mesh=mesh, in_specs=in_specs, out_specs=out_specs, check_vma=False)
```

profile of v0, /device:TPU:0, one launch (start us, length us, event | category | flops | bytes accessed | tf_op | source)
XLA Modules:
  0.0 265.4 jit_solution(16683940964910309810)
XLA Ops:
  7.2 0.0 copy-start
  7.2 0.0 reduce-scatter.4.cloned.1.call-start
  7.2 5.9 %collective-permute-start = (bf16[320,768]{1,0:T(8,128)(2,1)}, bf16[320,768]{1,0:T(8,128)(2,1)}, u32[]{:S(2)}, u32[]{:S(2)}) collective-permute-start(bf16[320,768]{1,0:T(8,128)(2,1)} %bitcast.74), channel_id=1, source_target_pairs={{0,2},{1,3},{2,4},{3,5},{4,6},{5,7},{8,10},{9,11},{10,12},{11,13},... | collective-permute-start | bytes 1474568 | tf_op jit(solution)/shard_map/ppermute | solution.py:19
  13.1 4.2 %collective-permute-start.1 = (bf16[320,768]{1,0:T(8,128)(2,1)}, bf16[320,768]{1,0:T(8,128)(2,1)}, u32[]{:S(2)}, u32[]{:S(2)}) collective-permute-start(bf16[320,768]{1,0:T(8,128)(2,1)} %bitcast.75), channel_id=1, source_target_pairs={{0,1},{1,2},{2,3},{3,4},{4,5},{5,6},{6,7},{8,9},{9,10},{10,11},{11... | collective-permute-start | bytes 1474568 | tf_op jit(solution)/shard_map/ppermute | solution.py:19
  17.3 2.7 %collective-permute-start.2 = (bf16[320,768]{1,0:T(8,128)(2,1)}, bf16[320,768]{1,0:T(8,128)(2,1)}, u32[]{:S(2)}, u32[]{:S(2)}) collective-permute-start(bf16[320,768]{1,0:T(8,128)(2,1)} %bitcast.76), channel_id=1, source_target_pairs={{0,2},{1,3},{2,4},{3,5},{4,6},{5,7},{8,10},{9,11},{10,12},{11,13},... | collective-permute-start | bytes 1474568 | tf_op jit(solution)/shard_map/ppermute | solution.py:19
  20.0 4.2 %collective-permute-start.3 = (bf16[320,768]{1,0:T(8,128)(2,1)}, bf16[320,768]{1,0:T(8,128)(2,1)}, u32[]{:S(2)}, u32[]{:S(2)}) collective-permute-start(bf16[320,768]{1,0:T(8,128)(2,1)} %bitcast.77), channel_id=1, source_target_pairs={{0,1},{1,2},{2,3},{3,4},{4,5},{5,6},{6,7},{8,9},{9,10},{10,11},{11... | collective-permute-start | bytes 1474568 | tf_op jit(solution)/shard_map/ppermute | solution.py:19
  24.3 1.3 copy.82
  25.6 1.3 copy.90
  26.9 1.3 constant_dynamic-slice_fusion
  28.9 1.3 copy.86
  30.3 0.3 copy.85
  30.6 0.3 copy.93
  30.9 1.3 copy.94
  32.9 0.1 pad_add_fusion
  33.0 1.3 copy.80
  34.3 1.0 copy.83
  35.4 1.3 copy.81
  36.7 1.0 copy.84
  37.7 1.3 copy.88
  39.1 1.0 copy.91
  40.1 1.3 copy.89
  41.5 1.0 copy.92
  42.5 5.6 %fusion.21 = f32[6,960,320]{1,2,0:T(8,128)} fusion(bf16[320,6,128]{0,2,1:T(8,128)(2,1)S(1)} %bitcast.65, bf16[320,6,128]{2,0,1:T(8,128)(2,1)S(1)} %copy.85, bf16[320,6,128]{2,0,1:T(8,128)(2,1)} %copy.84, bf16[320,6,128]{2,0,1:T(8,128)(2,1)} %copy.83), kind=kOutput, calls=%fused_computation.22 | convolution fusion | flops 476282880 | bytes 9338880 | tf_op jit(solution)/shard_map/qhd,khd->hqk/dot_general | solution.py:43
  48.1 11.5 %fusion.16 = f32[6,320,960]{2,1,0:T(8,128)} fusion(f32[6,960,320]{1,2,0:T(8,128)} %fusion.21, pred[960]{0:T(1024)(128)(4,1)S(1)} %pad_add_fusion), kind=kOutput, calls=%fused_computation.18 | output fusion | flops 11064958 | bytes 14746560 | tf_op jit(solution)/shard_map/div | solution.py:49
  59.6 4.4 %fusion.27 = f32[6,960,320]{1,2,0:T(8,128)} fusion(bf16[320,6,128]{0,2,1:T(8,128)(2,1)S(1)} %bitcast.67, bf16[320,6,128]{2,0,1:T(8,128)(2,1)S(1)} %copy.93, bf16[320,6,128]{2,0,1:T(8,128)(2,1)S(1)} %copy-done.2, bf16[320,6,128]{2,0,1:T(8,128)(2,1)S(1)} %copy-done.1), kind=kOutput, calls=%fused_computation.28 | convolution fusion | flops 476282880 | bytes 9338880 | tf_op jit(solution)/shard_map/qhd,khd->hqk/dot_general | solution.py:50
  64.0 14.1 %fusion.18 = f32[960,6,128]{2,0,1:T(8,128)} fusion(bf16[320,6,128]{0,2,1:T(8,128)(2,1)S(1)} %bitcast.66, f32[6,320,960]{2,1,0:T(8,128)} %fusion.16, f32[6,960,320]{1,2,0:T(8,128)} %fusion.27), kind=kOutput, calls=%fused_computation.20 | convolution fusion | flops 481078080 | bytes 18186240 | tf_op jit(solution)/shard_map/hqk,qhd->khd/dot_general | solution.py:53
  78.0 3.3 %fusion.44 = (f32[320,6,128]{2,0,1:T(8,128)S(1)}, f32[320,6,128]{2,0,1:T(8,128)}, f32[320,6,128]{2,0,1:T(8,128)}) fusion(f32[960,6,128]{2,0,1:T(8,128)} %fusion.18), kind=kLoop, calls=%fused_computation.51 | loop fusion | bytes 5898240 | tf_op jit(solution)/shard_map/slice | solution.py:100
  81.3 1.6 copy.98
  82.9 1.5 copy.99
  84.4 1.3 collective-permute-start.4
  85.7 1.6 copy.101
  87.3 1.3 copy.102
  88.6 1.3 collective-permute-start.5
  89.9 0.4 copy.97
  90.2 33.4 %collective-permute-done.4 = f32[320,768]{1,0:T(8,128)} collective-permute-done((f32[320,768]{1,0:T(8,128)}, f32[320,768]{1,0:T(8,128)}, u32[]{:S(2)}, u32[]{:S(2)}) %collective-permute-start.4) | collective-permute-done | bytes 983072 | tf_op jit(solution)/shard_map/ppermute | solution.py:19
  123.6 1.6 copy.100
  125.2 21.4 %collective-permute-done.5 = f32[320,768]{1,0:T(8,128)} collective-permute-done((f32[320,768]{1,0:T(8,128)}, f32[320,768]{1,0:T(8,128)}, u32[]{:S(2)}, u32[]{:S(2)}) %collective-permute-start.5) | collective-permute-done | bytes 983072 | tf_op jit(solution)/shard_map/ppermute | solution.py:19
  146.6 2.6 copy.103
  149.2 1.4 fusion.34
  150.6 0.8 convolution_bitcast_fusion
  151.4 0.0 copy-start.3
  151.4 2.0 copy.108
  153.4 0.0 reduce-scatter.4.cloned.1.call-update
  153.4 0.0 all-reduce.2.cloned.1.call-start
  153.5 69.0 %reduce-scatter.4.cloned.1.call-done = f32[96,768]{1,0:T(8,128)} async-done(((f32[768,768]{1,0:T(8,128)}), f32[96,768]{1,0:T(8,128)}) %reduce-scatter.4.cloned.1.call-update) | async-done | bytes 294928 | tf_op jit(solution)/shard_map/reduce_scatter | solution.py:106
  222.5 0.0 all-reduce.2.cloned.1.call-update
  222.5 33.9 %all-reduce.2.cloned.1.call-done = f32[96,768]{1,0:T(8,128)} async-done(((f32[96,768]{1,0:T(8,128)}), f32[96,768]{1,0:T(8,128)}) %all-reduce.2.cloned.1.call-update) | async-done | bytes 294928 | tf_op jit(solution)/shard_map/psum | solution.py:109
  256.4 2.1 multiply_subtract_fusion
  (15 shorter events, 0.0 us)
Async XLA Ops:
  7.2 143.5 %copy-start = (bf16[1,320,768]{2,1,0:T(8,128)(2,1)S(1)}, bf16[1,320,768]{2,1,0:T(8,128)(2,1)}, u32[]{:S(2)}) copy-start(bf16[1,320,768]{2,1,0:T(8,128)(2,1)} %param.9) | copy-start | bytes 1474564
  7.2 215.3 %reduce-scatter.4.cloned.1.call-start = ((), (), s32[]{:S(2)}) async-start(), calls=%async_computation.2 | async-start | bytes 2654208 | tf_op jit(solution)/shard_map/reduce_scatter | solution.py:106
  7.2 25.8 %collective-permute-start = (bf16[320,768]{1,0:T(8,128)(2,1)}, bf16[320,768]{1,0:T(8,128)(2,1)}, u32[]{:S(2)}, u32[]{:S(2)}) collective-permute-start(bf16[320,768]{1,0:T(8,128)(2,1)} %bitcast.74), channel_id=1, source_target_pairs={{0,2},{1,3},{2,4},{3,5},{4,6},{5,7},{8,10},{9,11},{10,12},{11,13},... | collective-permute-start | bytes 1474568 | tf_op jit(solution)/shard_map/ppermute | solution.py:19
  13.1 22.3 %collective-permute-start.1 = (bf16[320,768]{1,0:T(8,128)(2,1)}, bf16[320,768]{1,0:T(8,128)(2,1)}, u32[]{:S(2)}, u32[]{:S(2)}) collective-permute-start(bf16[320,768]{1,0:T(8,128)(2,1)} %bitcast.75), channel_id=1, source_target_pairs={{0,1},{1,2},{2,3},{3,4},{4,5},{5,6},{6,7},{8,9},{9,10},{10,11},{11... | collective-permute-start | bytes 1474568 | tf_op jit(solution)/shard_map/ppermute | solution.py:19
  17.3 20.4 %collective-permute-start.2 = (bf16[320,768]{1,0:T(8,128)(2,1)}, bf16[320,768]{1,0:T(8,128)(2,1)}, u32[]{:S(2)}, u32[]{:S(2)}) collective-permute-start(bf16[320,768]{1,0:T(8,128)(2,1)} %bitcast.76), channel_id=1, source_target_pairs={{0,2},{1,3},{2,4},{3,5},{4,6},{5,7},{8,10},{9,11},{10,12},{11,13},... | collective-permute-start | bytes 1474568 | tf_op jit(solution)/shard_map/ppermute | solution.py:19
  20.0 20.1 %collective-permute-start.3 = (bf16[320,768]{1,0:T(8,128)(2,1)}, bf16[320,768]{1,0:T(8,128)(2,1)}, u32[]{:S(2)}, u32[]{:S(2)}) collective-permute-start(bf16[320,768]{1,0:T(8,128)(2,1)} %bitcast.77), channel_id=1, source_target_pairs={{0,1},{1,2},{2,3},{3,4},{4,5},{5,6},{6,7},{8,9},{9,10},{10,11},{11... | collective-permute-start | bytes 1474568 | tf_op jit(solution)/shard_map/ppermute | solution.py:19
  48.1 11.5 %copy-start.1 = (bf16[320,6,128]{2,0,1:T(8,128)(2,1)S(1)}, bf16[320,6,128]{2,0,1:T(8,128)(2,1)}, u32[]{:S(2)}) copy-start(bf16[320,6,128]{2,0,1:T(8,128)(2,1)} %copy.91) | copy-start | bytes 1474564
  48.1 11.5 %copy-start.2 = (bf16[320,6,128]{2,0,1:T(8,128)(2,1)S(1)}, bf16[320,6,128]{2,0,1:T(8,128)(2,1)}, u32[]{:S(2)}) copy-start(bf16[320,6,128]{2,0,1:T(8,128)(2,1)} %copy.92) | copy-start | bytes 1474564
  84.4 39.2 %collective-permute-start.4 = (f32[320,768]{1,0:T(8,128)}, f32[320,768]{1,0:T(8,128)}, u32[]{:S(2)}, u32[]{:S(2)}) collective-permute-start(f32[320,768]{1,0:T(8,128)} %copy.99), channel_id=1, source_target_pairs={{1,0},{2,1},{3,2},{4,3},{5,4},{6,5},{7,6},{9,8},{10,9},{11,10},{12... | collective-permute-start | bytes 2949128 | tf_op jit(solution)/shard_map/ppermute | solution.py:19
  88.6 58.0 %collective-permute-start.5 = (f32[320,768]{1,0:T(8,128)}, f32[320,768]{1,0:T(8,128)}, u32[]{:S(2)}, u32[]{:S(2)}) collective-permute-start(f32[320,768]{1,0:T(8,128)} %copy.102), channel_id=1, source_target_pairs={{2,0},{3,1},{4,2},{5,3},{6,4},{7,5},{10,8},{11,9},{12,10},{13,11},... | collective-permute-start | bytes 2949128 | tf_op jit(solution)/shard_map/ppermute | solution.py:19
  151.4 105.0 %copy-start.3 = (f32[96,768]{1,0:T(8,128)S(1)}, f32[96,768]{1,0:T(8,128)}, u32[]{:S(2)}) copy-start(f32[96,768]{1,0:T(8,128)} %param.15) | copy-start | bytes 884740
  151.4 105.0 %copy-start.4 = (f32[96,768]{1,0:T(8,128)S(1)}, f32[96,768]{1,0:T(8,128)}, u32[]{:S(2)}) copy-start(f32[96,768]{1,0:T(8,128)} %param.16) | copy-start | bytes 884740
  153.4 103.0 %all-reduce.2.cloned.1.call-start = ((), (), s32[]{:S(2)}) async-start(), calls=%async_computation.1 | async-start | bytes 589824 | tf_op jit(solution)/shard_map/psum | solution.py:109
Sparse Core Ops, SparseCore 0:
  153.5 68.8 reduce-scatter.3
  224.8 31.5 all-reduce.1
where the time goes:
time: 266 us; the launch traced here: 265 us
  waiting for transfers between devices  158 us (59%)
  local copies, waits for them, and re-layouts  32.5 us (12%)
  matrix products  24.8 us (9%)
  starting transfers between devices  19.7 us (7%)
  between operations  15.5 us (6%)
  other arithmetic  15.1 us (6%)
    reduce_scatter x1, waiting for transfers between devices, body(): lax.psum_scatter(contract_rows(features, key_grad), 'tm', scatter_dimensi...  69 us
    ppermute x6, waiting for transfers between devices, from_behind(): lax.ppermute(value, axis, [(source, source + steps) for source in range(l...  54.8 us
    psum x1, waiting for transfers between devices, body(): gradient = lax.psum(local_rows, 'clip')  33.9 us
    ppermute x6, starting transfers between devices, from_behind(): lax.ppermute(value, axis, [(source, source + steps) for source in range(l...  19.6 us
    dot_general x1, matrix products, window_grad(): jnp.einsum('hqk,qhd->khd', dscores, query_heads, preferred_element_type=j...  14.1 us
    div x1, other arithmetic, window_grad(): softmax = raised / jnp.sum(raised, axis=-1, keepdims=True)  11.5 us
    ppermute x6, local copies, waits for them, and re-layouts, from_behind(): lax.ppermute(value, axis, [(source, source + steps) for source in range(l...  9.48 us
    unnamed x15, local copies, waits for them, and re-layouts  7.34 us
  transfers between devices with their start and end apart: 8, of which 4 were waited for; matrix products, arithmetic and copies ran while one was open for 7% of the time, Pallas kernels for 0%

commit v1 on v0

--- a/solution.py
+++ b/solution.py
@@ -11,6 +11,10 @@
 adam_eps = 1e-08
 decay_rate = 0.1
 step_count = 10.0
+
+
+def _pack_sites(page):
+    return lax.all_gather(page, axis_name="clip").sum(axis=0)
 
 
 def from_behind(value, axis, steps):
@@ -106,7 +110,7 @@
     local_rows = lax.psum_scatter(
         contract_rows(features, key_grad), "tm", scatter_dimension=0, tiled=True
     )
-    gradient = lax.psum(local_rows, "clip")
+    gradient = _pack_sites(local_rows)
     return adamw(weight, moment_one, moment_two, gradient)
 
 

time: 266 us -> 251 us (0.944)
  waiting for transfers between devices: 158 us -> 142 us
    psum x1 -> x0, waiting for transfers between devices: 33.9 us -> none  [body(): gradient = lax.psum(local_rows, 'clip')]
    all_gather x0 -> x1, waiting for transfers between devices: none -> 18.2 us  [_pack_sites(): return lax.all_gather(page, axis_name='clip').sum(axis=0)]
    unnamed x15 -> x17, local copies, waits for them, and re-layouts: 7.34 us -> 7.33 us
  transfers between devices with their start and end apart: 8 -> 8, of which waited for: 4 -> 4; matrix products, arithmetic and copies ran while one was open for 7% -> 8% of each run, Pallas kernels for 0% -> 0%
where the time goes in v1:
time: 251 us; the launch traced here: 250 us
  waiting for transfers between devices  142 us (57%)
  local copies, waits for them, and re-layouts  32.5 us (13%)
  matrix products  24.8 us (10%)
  starting transfers between devices  19.7 us (8%)
  between operations  15.5 us (6%)
  other arithmetic  15.4 us (6%)
    reduce_scatter x1, waiting for transfers between devices, body(): lax.psum_scatter(contract_rows(features, key_grad), 'tm', scatter_dimensi...  69.2 us
    ppermute x6, waiting for transfers between devices, from_behind(): lax.ppermute(value, axis, [(source, source + steps) for source in range(l...  54.8 us
    ppermute x6, starting transfers between devices, from_behind(): lax.ppermute(value, axis, [(source, source + steps) for source in range(l...  19.6 us
    all_gather x1, waiting for transfers between devices, _pack_sites(): return lax.all_gather(page, axis_name='clip').sum(axis=0)  18.2 us
    dot_general x1, matrix products, window_grad(): jnp.einsum('hqk,qhd->khd', dscores, query_heads, preferred_element_type=j...  14.1 us
    div x1, other arithmetic, window_grad(): softmax = raised / jnp.sum(raised, axis=-1, keepdims=True)  11.5 us
    ppermute x6, local copies, waits for them, and re-layouts, from_behind(): lax.ppermute(value, axis, [(source, source + steps) for source in range(l...  9.48 us
    unnamed x17, local copies, waits for them, and re-layouts  7.33 us
  transfers between devices with their start and end apart: 8, of which 4 were waited for; matrix products, arithmetic and copies ran while one was open for 8% of the time, Pallas kernels for 0%

profile of v1, /device:TPU:0, one launch (start us, length us, event | category | flops | bytes accessed | tf_op | source)
XLA Modules:
  0.0 250.1 jit_solution(7545622890301986368)
XLA Ops:
  7.2 0.0 copy-start
  7.2 0.0 reduce-scatter.4.cloned.1.call-start
  7.2 5.9 %collective-permute-start = (bf16[320,768]{1,0:T(8,128)(2,1)}, bf16[320,768]{1,0:T(8,128)(2,1)}, u32[]{:S(2)}, u32[]{:S(2)}) collective-permute-start(bf16[320,768]{1,0:T(8,128)(2,1)} %bitcast.76), channel_id=1, source_target_pairs={{0,2},{1,3},{2,4},{3,5},{4,6},{5,7},{8,10},{9,11},{10,12},{11,13},... | collective-permute-start | bytes 1474568 | tf_op jit(solution)/shard_map/ppermute | solution.py:23
  13.1 4.2 %collective-permute-start.1 = (bf16[320,768]{1,0:T(8,128)(2,1)}, bf16[320,768]{1,0:T(8,128)(2,1)}, u32[]{:S(2)}, u32[]{:S(2)}) collective-permute-start(bf16[320,768]{1,0:T(8,128)(2,1)} %bitcast.77), channel_id=1, source_target_pairs={{0,1},{1,2},{2,3},{3,4},{4,5},{5,6},{6,7},{8,9},{9,10},{10,11},{11... | collective-permute-start | bytes 1474568 | tf_op jit(solution)/shard_map/ppermute | solution.py:23
  17.3 2.8 %collective-permute-start.2 = (bf16[320,768]{1,0:T(8,128)(2,1)}, bf16[320,768]{1,0:T(8,128)(2,1)}, u32[]{:S(2)}, u32[]{:S(2)}) collective-permute-start(bf16[320,768]{1,0:T(8,128)(2,1)} %bitcast.78), channel_id=1, source_target_pairs={{0,2},{1,3},{2,4},{3,5},{4,6},{5,7},{8,10},{9,11},{10,12},{11,13},... | collective-permute-start | bytes 1474568 | tf_op jit(solution)/shard_map/ppermute | solution.py:23
  20.0 4.2 %collective-permute-start.3 = (bf16[320,768]{1,0:T(8,128)(2,1)}, bf16[320,768]{1,0:T(8,128)(2,1)}, u32[]{:S(2)}, u32[]{:S(2)}) collective-permute-start(bf16[320,768]{1,0:T(8,128)(2,1)} %bitcast.79), channel_id=1, source_target_pairs={{0,1},{1,2},{2,3},{3,4},{4,5},{5,6},{6,7},{8,9},{9,10},{10,11},{11... | collective-permute-start | bytes 1474568 | tf_op jit(solution)/shard_map/ppermute | solution.py:23
  24.3 1.3 copy.38
  25.6 1.3 copy.46
  27.0 1.3 constant_dynamic-slice_fusion
  28.9 1.3 copy.42
  30.3 0.3 copy.41
  30.6 0.3 copy.49
  30.9 1.3 copy.50
  32.9 0.1 pad_add_fusion
  33.0 1.3 copy.36
  34.4 1.0 copy.39
  35.4 1.3 copy.37
  36.7 1.0 copy.40
  37.8 1.3 copy.44
  39.1 1.0 copy.47
  40.1 1.3 copy.45
  41.5 1.0 copy.48
  42.5 5.6 %fusion.21 = f32[6,960,320]{1,2,0:T(8,128)} fusion(bf16[320,6,128]{0,2,1:T(8,128)(2,1)S(1)} %bitcast.66, bf16[320,6,128]{2,0,1:T(8,128)(2,1)S(1)} %copy.41, bf16[320,6,128]{2,0,1:T(8,128)(2,1)} %copy.40, bf16[320,6,128]{2,0,1:T(8,128)(2,1)} %copy.39), kind=kOutput, calls=%fused_computation.22 | convolution fusion | flops 476282880 | bytes 9338880 | tf_op jit(solution)/shard_map/qhd,khd->hqk/dot_general | solution.py:47
  48.1 11.5 %fusion.16 = f32[6,320,960]{2,1,0:T(8,128)} fusion(f32[6,960,320]{1,2,0:T(8,128)} %fusion.21, pred[960]{0:T(1024)(128)(4,1)S(1)} %pad_add_fusion), kind=kOutput, calls=%fused_computation.18 | output fusion | flops 11064958 | bytes 14746560 | tf_op jit(solution)/shard_map/div | solution.py:53
  59.6 4.4 %fusion.27 = f32[6,960,320]{1,2,0:T(8,128)} fusion(bf16[320,6,128]{0,2,1:T(8,128)(2,1)S(1)} %bitcast.68, bf16[320,6,128]{2,0,1:T(8,128)(2,1)S(1)} %copy.49, bf16[320,6,128]{2,0,1:T(8,128)(2,1)S(1)} %copy-done.2, bf16[320,6,128]{2,0,1:T(8,128)(2,1)S(1)} %copy-done.1), kind=kOutput, calls=%fused_computation.28 | convolution fusion | flops 476282880 | bytes 9338880 | tf_op jit(solution)/shard_map/qhd,khd->hqk/dot_general | solution.py:54
  64.0 14.1 %fusion.18 = f32[960,6,128]{2,0,1:T(8,128)} fusion(bf16[320,6,128]{0,2,1:T(8,128)(2,1)S(1)} %bitcast.67, f32[6,320,960]{2,1,0:T(8,128)} %fusion.16, f32[6,960,320]{1,2,0:T(8,128)} %fusion.27), kind=kOutput, calls=%fused_computation.20 | convolution fusion | flops 481078080 | bytes 18186240 | tf_op jit(solution)/shard_map/hqk,qhd->khd/dot_general | solution.py:57
  78.0 3.3 %fusion.44 = (f32[320,6,128]{2,0,1:T(8,128)S(1)}, f32[320,6,128]{2,0,1:T(8,128)}, f32[320,6,128]{2,0,1:T(8,128)}) fusion(f32[960,6,128]{2,0,1:T(8,128)} %fusion.18), kind=kLoop, calls=%fused_computation.51 | loop fusion | bytes 5898240 | tf_op jit(solution)/shard_map/slice | solution.py:104
  81.4 1.6 copy.54
  82.9 1.5 copy.55
  84.4 1.3 collective-permute-start.4
  85.7 1.6 copy.57
  87.3 1.3 copy.58
  88.6 1.3 collective-permute-start.5
  89.9 0.4 copy.53
  90.3 33.3 %collective-permute-done.4 = f32[320,768]{1,0:T(8,128)} collective-permute-done((f32[320,768]{1,0:T(8,128)}, f32[320,768]{1,0:T(8,128)}, u32[]{:S(2)}, u32[]{:S(2)}) %collective-permute-start.4) | collective-permute-done | bytes 983072 | tf_op jit(solution)/shard_map/ppermute | solution.py:23
  123.6 1.6 copy.56
  125.2 21.4 %collective-permute-done.5 = f32[320,768]{1,0:T(8,128)} collective-permute-done((f32[320,768]{1,0:T(8,128)}, f32[320,768]{1,0:T(8,128)}, u32[]{:S(2)}, u32[]{:S(2)}) %collective-permute-start.5) | collective-permute-done | bytes 983072 | tf_op jit(solution)/shard_map/ppermute | solution.py:23
  146.6 2.6 %copy.59 = f32[320,768]{0,1:T(8,128)} copy(f32[320,768]{1,0:T(8,128)} %collective-permute-done.5) | data formatting | bytes 1966080 | tf_op jit(solution)/shard_map/ppermute | solution.py:23
  149.2 1.4 fusion.34
  150.6 0.8 convolution_bitcast_fusion
  151.4 2.0 copy.64
  153.4 0.0 reduce-scatter.4.cloned.1.call-update
  153.4 0.0 all-gather.3.cloned.1.call-start
  153.4 69.2 %reduce-scatter.4.cloned.1.call-done = f32[96,768]{1,0:T(8,128)} async-done(((f32[768,768]{1,0:T(8,128)}), f32[96,768]{1,0:T(8,128)}) %reduce-scatter.4.cloned.1.call-update) | async-done | bytes 294928 | tf_op jit(solution)/shard_map/reduce_scatter | solution.py:110
  222.6 0.0 all-gather.3.cloned.1.call-update
  222.6 18.2 %all-gather.3.cloned.1.call-done = f32[384,768]{1,0:T(8,128)} async-done(((f32[96,768]{1,0:T(8,128)}), f32[384,768]{1,0:T(8,128)}) %all-gather.3.cloned.1.call-update) | async-done | bytes 1179664 | tf_op jit(solution)/shard_map/all_gather | solution.py:17
  240.9 1.4 reduce_sum.29
  242.3 1.0 multiply_subtract_fusion
  (18 shorter events, 0.0 us)
Async XLA Ops:
  7.2 143.5 %copy-start = (bf16[1,320,768]{2,1,0:T(8,128)(2,1)S(1)}, bf16[1,320,768]{2,1,0:T(8,128)(2,1)}, u32[]{:S(2)}) copy-start(bf16[1,320,768]{2,1,0:T(8,128)(2,1)} %param.9) | copy-start | bytes 1474564
  7.2 215.4 %reduce-scatter.4.cloned.1.call-start = ((), (), s32[]{:S(2)}) async-start(), calls=%async_computation.2 | async-start | bytes 2654208 | tf_op jit(solution)/shard_map/reduce_scatter | solution.py:110
  7.2 25.8 %collective-permute-start = (bf16[320,768]{1,0:T(8,128)(2,1)}, bf16[320,768]{1,0:T(8,128)(2,1)}, u32[]{:S(2)}, u32[]{:S(2)}) collective-permute-start(bf16[320,768]{1,0:T(8,128)(2,1)} %bitcast.76), channel_id=1, source_target_pairs={{0,2},{1,3},{2,4},{3,5},{4,6},{5,7},{8,10},{9,11},{10,12},{11,13},... | collective-permute-start | bytes 1474568 | tf_op jit(solution)/shard_map/ppermute | solution.py:23
  13.1 22.3 %collective-permute-start.1 = (bf16[320,768]{1,0:T(8,128)(2,1)}, bf16[320,768]{1,0:T(8,128)(2,1)}, u32[]{:S(2)}, u32[]{:S(2)}) collective-permute-start(bf16[320,768]{1,0:T(8,128)(2,1)} %bitcast.77), channel_id=1, source_target_pairs={{0,1},{1,2},{2,3},{3,4},{4,5},{5,6},{6,7},{8,9},{9,10},{10,11},{11... | collective-permute-start | bytes 1474568 | tf_op jit(solution)/shard_map/ppermute | solution.py:23
  17.3 20.5 %collective-permute-start.2 = (bf16[320,768]{1,0:T(8,128)(2,1)}, bf16[320,768]{1,0:T(8,128)(2,1)}, u32[]{:S(2)}, u32[]{:S(2)}) collective-permute-start(bf16[320,768]{1,0:T(8,128)(2,1)} %bitcast.78), channel_id=1, source_target_pairs={{0,2},{1,3},{2,4},{3,5},{4,6},{5,7},{8,10},{9,11},{10,12},{11,13},... | collective-permute-start | bytes 1474568 | tf_op jit(solution)/shard_map/ppermute | solution.py:23
  20.0 20.1 %collective-permute-start.3 = (bf16[320,768]{1,0:T(8,128)(2,1)}, bf16[320,768]{1,0:T(8,128)(2,1)}, u32[]{:S(2)}, u32[]{:S(2)}) collective-permute-start(bf16[320,768]{1,0:T(8,128)(2,1)} %bitcast.79), channel_id=1, source_target_pairs={{0,1},{1,2},{2,3},{3,4},{4,5},{5,6},{6,7},{8,9},{9,10},{10,11},{11... | collective-permute-start | bytes 1474568 | tf_op jit(solution)/shard_map/ppermute | solution.py:23
  48.1 11.5 %copy-start.1 = (bf16[320,6,128]{2,0,1:T(8,128)(2,1)S(1)}, bf16[320,6,128]{2,0,1:T(8,128)(2,1)}, u32[]{:S(2)}) copy-start(bf16[320,6,128]{2,0,1:T(8,128)(2,1)} %copy.47) | copy-start | bytes 1474564
  48.1 11.5 %copy-start.2 = (bf16[320,6,128]{2,0,1:T(8,128)(2,1)S(1)}, bf16[320,6,128]{2,0,1:T(8,128)(2,1)}, u32[]{:S(2)}) copy-start(bf16[320,6,128]{2,0,1:T(8,128)(2,1)} %copy.48) | copy-start | bytes 1474564
  84.4 39.2 %collective-permute-start.4 = (f32[320,768]{1,0:T(8,128)}, f32[320,768]{1,0:T(8,128)}, u32[]{:S(2)}, u32[]{:S(2)}) collective-permute-start(f32[320,768]{1,0:T(8,128)} %copy.55), channel_id=1, source_target_pairs={{1,0},{2,1},{3,2},{4,3},{5,4},{6,5},{7,6},{9,8},{10,9},{11,10},{12... | collective-permute-start | bytes 2949128 | tf_op jit(solution)/shard_map/ppermute | solution.py:23
  88.6 58.0 %collective-permute-start.5 = (f32[320,768]{1,0:T(8,128)}, f32[320,768]{1,0:T(8,128)}, u32[]{:S(2)}, u32[]{:S(2)}) collective-permute-start(f32[320,768]{1,0:T(8,128)} %copy.58), channel_id=1, source_target_pairs={{2,0},{3,1},{4,2},{5,3},{6,4},{7,5},{10,8},{11,9},{12,10},{13,11},... | collective-permute-start | bytes 2949128 | tf_op jit(solution)/shard_map/ppermute | solution.py:23
  153.4 88.9 %copy-start.3 = (f32[96,768]{1,0:T(8,128)S(1)}, f32[96,768]{1,0:T(8,128)}, u32[]{:S(2)}) copy-start(f32[96,768]{1,0:T(8,128)} %param.15) | copy-start | bytes 884740
  153.4 88.9 %copy-start.4 = (f32[96,768]{1,0:T(8,128)S(1)}, f32[96,768]{1,0:T(8,128)}, u32[]{:S(2)}) copy-start(f32[96,768]{1,0:T(8,128)} %param.16) | copy-start | bytes 884740
  153.4 88.9 %copy-start.5 = (f32[96,768]{1,0:T(8,128)S(1)}, f32[96,768]{1,0:T(8,128)}, u32[]{:S(2)}) copy-start(f32[96,768]{1,0:T(8,128)} %param.17) | copy-start | bytes 884740
  153.4 87.5 %all-gather.3.cloned.1.call-start = ((), (), s32[]{:S(2)}) async-start(), calls=%async_computation.1 | async-start | bytes 1474560 | tf_op jit(solution)/shard_map/all_gather | solution.py:17
Sparse Core Ops, SparseCore 0:
  153.5 69.0 reduce-scatter.3
  224.2 16.6 all-gather.2
